TPU v7x, 32 devices: a whole 2x2x4 slice. The times are simulated.
32 devices in a mesh: tgt: 4 (over y, x), sup: 8 (over z, core).
Axes of the slice: x: 2, y: 2, z: 4, core: 2. Of those that a mesh axis runs over, the one named last changes fastest.
Arguments:
- support: float32 [32, 3, 1024], P(('sup', 'tgt')), may hold values from -14 to 14
- coeffs: float32 [32, 100], P('sup'), may hold values from -10 to 10
- targets: float32 [32, 3, 1024], P(('tgt', 'sup')), may hold values from -14 to 14
- labels: float32 [32, 100], P(('tgt', 'sup')), may hold values from -5 to 5
Outputs:
- support_grad: float32 [32, 3, 1024], P(('sup', 'tgt'))
- residual: float32 [32, 100], P(('tgt', 'sup'))
All inputs are finite; a program needn't handle non-finite values.
Results may differ from a plain program's by a relative error of at most 0.000064.
Values sent between devices are 32-bit elements; how exact they have to be, the bound alone decides.
No kernel may reach another device: no remote copies, remote signals or barrier semaphores. Data moves between devices by JAX's collectives and lax.ppermute only.
A program may use at most 128 MiB of HBM per device.

v0:
```python
import math
import jax
import jax.numpy as jnp
from jax import lax
from jax.sharding import PartitionSpec as P

SIDE = 32
DEPTH = 3
WEIGHT_VAR = 1.6
BIAS_VAR = 0.1


def spread(values):
    side_cells = values.shape[0]
    padded = jnp.pad(values, ((1, 1), (1, 1), (0, 0)))
    summed = jnp.zeros_like(values)
    for row_shift in range(3):
        for col_shift in range(3):
            summed = (
                summed
                + padded[row_shift : row_shift + side_cells, col_shift : col_shift + side_cells]
            )
    return summed / 9.0


def self_levels(images):
    image_count = images.shape[0]
    energy = jnp.mean(images * images, axis=1)
    kernel_level = WEIGHT_VAR * spread(energy.T.reshape(SIDE, SIDE, image_count)) + BIAS_VAR
    levels = [kernel_level]
    for layer_idx in range(DEPTH - 1):
        activated = 2.0 / math.pi * jnp.arcsin(2.0 * kernel_level / (1.0 + 2.0 * kernel_level))
        kernel_level = WEIGHT_VAR * spread(activated) + BIAS_VAR
        levels.append(kernel_level)
    return levels


def pair_kernel(support, targets):
    sup_count = support.shape[0]
    tgt_count = targets.shape[0]
    sup_levels = self_levels(support)
    tgt_levels = self_levels(targets)
    products = (
        jnp.einsum("scp,tcp->pst", support, targets, precision=lax.Precision.HIGHEST)
        / support.shape[1]
    )
    kernel_level = (
        WEIGHT_VAR * spread(products.reshape(SIDE, SIDE, sup_count * tgt_count)) + BIAS_VAR
    )
    activated = kernel_level
    for layer_idx in range(DEPTH):
        sup_gain = lax.rsqrt(1.0 + 2.0 * sup_levels[layer_idx])
        tgt_gain = lax.rsqrt(1.0 + 2.0 * tgt_levels[layer_idx])
        correlation = (
            2.0
            * kernel_level.reshape(SIDE, SIDE, sup_count, tgt_count)
            * sup_gain[:, :, :, None]
            * tgt_gain[:, :, None, :]
        )
        activated = 2.0 / math.pi * jnp.arcsin(correlation)
        if layer_idx + 1 < DEPTH:
            kernel_level = (
                WEIGHT_VAR * spread(activated.reshape(SIDE, SIDE, sup_count * tgt_count)) + BIAS_VAR
            )
    return WEIGHT_VAR * jnp.mean(activated, axis=(0, 1)) + BIAS_VAR


def product(left, right):
    return jnp.dot(left, right, precision=lax.Precision.HIGHEST, preferred_element_type=jnp.float32)


def local(support, coeffs, targets, labels):
    tgt_dev = targets.shape[0]
    block = lax.all_gather(support, "tgt", axis=0, tiled=True)
    group, group_labels = (
        lax.all_gather(targets, "sup", axis=0, tiled=True),
        lax.all_gather(labels, "sup", axis=0, tiled=True),
    )
    theta, pullback = jax.vjp(lambda images: pair_kernel(images, group), block)
    predicted = lax.psum(product(theta.T, coeffs), "sup")
    misfit = predicted - group_labels
    residual = lax.dynamic_slice_in_dim(misfit, lax.axis_index("sup") * tgt_dev, tgt_dev, 0)
    block_grad = pullback(product(coeffs, misfit.T))[0]
    support_grad = lax.psum_scatter(block_grad, "tgt", scatter_dimension=0, tiled=True)
    return (support_grad, residual)


def solution(mesh):
    return jax.shard_map(
        local,
        mesh=mesh,
        in_specs=(
            P(("sup", "tgt"), None, None),
            P("sup", None),
            P(("tgt", "sup"), None, None),
            P(("tgt", "sup"), None),
        ),
        out_specs=(P(("sup", "tgt"), None, None), P(("tgt", "sup"), None)),
        check_vma=False,
    )
```

profile of v0, /device:TPU:0, one launch (start us, length us, event | category | flops | bytes accessed | tf_op | source)
XLA Modules:
  0.0 127.9 jit_solution(11291109133535098446)
XLA Ops:
  0.7 0.7 copy.146
  1.4 9.7 %all_gather.9 = f32[4,3,1024]{2,1,0:T(4,128)S(1)} all-gather(f32[1,3,1024]{2,1,0:T(4,128)S(1)} %copy.146), channel_id=1, replica_groups=mesh['tgt'=4,'sup'=8] {'tgt'}, dimensions={0}, use_global_device_ids=true | all-gather | bytes 61440 | tf_op jit(solution)/shard_map/all_gather | solution.py:74
  12.0 14.3 %all_gather.10 = f32[8,3,1024]{2,1,0:T(4,128)S(1)} all-gather(f32[1,3,1024]{2,1,0:T(4,128)S(1)} %copy.147), channel_id=1, replica_groups=mesh['tgt'=4,'sup'=8] {'sup'}, dimensions={0}, use_global_device_ids=true | all-gather | bytes 110592 | tf_op jit(solution)/shard_map/all_gather | solution.py:76
  26.8 0.9 add_rsqrt_fusion.1
  27.9 2.7 %copy.149 = f32[8,3,1024]{1,0,2:T(8,128)} copy(f32[8,3,1024]{2,1,0:T(4,128)S(1)} %all_gather.10) | data formatting | bytes 196608 | tf_op jit(solution)/shard_map/all_gather | solution.py:76
  30.6 1.8 %copy.148 = f32[4,3,1024]{1,0,2:T(4,128)} copy(f32[4,3,1024]{2,1,0:T(4,128)S(1)} %all_gather.9) | data formatting | bytes 98304 | tf_op jit(solution)/shard_map/all_gather | solution.py:74
  32.4 9.7 %convolution_multiply_fusion = f32[1024,4,8]{2,1,0:T(4,128)S(1)} fusion(f32[4,3,1024]{1,0,2:T(4,128)} %copy.148, f32[8,3,1024]{1,0,2:T(8,128)} %copy.149), kind=kOutput, calls=%fused_computation | convolution fusion | flops 1212416 | bytes 278528 | tf_op jit(solution)/shard_map/jvp(scp,tcp->pst)/dot_general | solution.py:44
  42.1 0.9 copy.150
  43.2 2.7 %add_multiply_fusion.3 = (f32[32,32,32]{1,0,2:T(8,128)S(1)}, f32[32,32,32]{1,0,2:T(8,128)S(1)}) fusion(f32[32,32,32]{1,2,0:T(8,128)S(1)} %get-tuple-element.40, f32[32,32,32]{1,2,0:T(8,128)S(1)} %get-tuple-element.41, f32[32,32,32]{1,0,2:T(8,128)S(1)} %reshape.78), kind=kLoop, calls=%fused_computation.116 | loop fusion | flops 589824 | bytes 655360 | tf_op jit(solution)/shard_map/jvp()/mul | solution.py:60
  45.9 0.7 add_multiply_fusion.11
  47.7 3.3 %add_multiply_fusion.1 = (f32[32,32,32]{1,0,2:T(8,128)S(1)}, f32[32,32,32]{1,0,2:T(8,128)}) fusion(f32[32,32,32]{1,2,0:T(8,128)S(1)} %get-tuple-element.42, f32[32,32,32]{1,2,0:T(8,128)S(1)} %get-tuple-element.43, f32[32,32,32]{1,0,2:T(8,128)S(1)} %get-tuple-element.26), kind=kLoop, calls=%fused_computation.114 | loop fusion | flops 589824 | bytes 655360 | tf_op jit(solution)/shard_map/jvp()/mul | solution.py:60
  51.0 0.7 add_multiply_fusion.9
  51.7 0.8 broadcast_multiply_fusion.2
  53.4 2.3 %multiply_reduce_fusion = (f32[32]{0:T(128)S(1)}, f32[32,32,32]{1,0,2:T(8,128)S(1)}) fusion(f32[32,32,32]{1,2,0:T(8,128)S(1)} %get-tuple-element.44, f32[32,32,32]{1,2,0:T(8,128)S(1)} %get-tuple-element.45, f32[32,32,32]{1,0,2:T(8,128)S(1)} %get-tuple-element.22), kind=kLoop, calls=%fused_computation.112 | loop fusion | flops 622560 | bytes 524416 | tf_op jit(solution)/shard_map/jvp()/reduce_sum | solution.py:65
  55.9 16.9 %psum.7 = f32[8,100]{1,0:T(8,128)S(1)} all-reduce(f32[8,100]{1,0:T(8,128)S(1)} %fusion.155), channel_id=1, replica_groups=mesh['tgt'=4,'sup'=8] {'sup'}, use_global_device_ids=true, to_apply=%region_3.4 | all-reduce | flops 800 | bytes 6400 | tf_op jit(solution)/shard_map/psum | solution.py:80
  72.8 8.6 %all-gather = f32[8,1,100]{2,1,0:T(1,128)S(1)} all-gather(f32[1,1,100]{2,1,0:T(1,128)S(1)} %bitcast.95), channel_id=1, replica_groups=mesh['tgt'=4,'sup'=8] {'sup'}, dimensions={0}, use_global_device_ids=true | all-gather | bytes 3600 | tf_op jit(solution)/shard_map/all_gather | solution.py:77
  81.6 1.4 %fusion.35 = f32[32,32,4]{1,2,0:T(4,128)S(1)} fusion(f32[32,32,32]{1,0,2:T(8,128)S(1)} %get-tuple-element.19, f32[4,8]{1,0:T(4,128)S(1)} %fusion, f32[32,32,8]{1,2,0:T(8,128)S(1)} %copy.169, f32[32,32,4]{1,2,0:T(4,128)} %copy-done.16), kind=kLoop, calls=%fused_computation.84 | loop fusion | flops 323584 | bytes 196736 | tf_op jit(solution)/shard_map/transpose(jvp())/reduce_sum | solution.py:55
  83.0 0.9 fusion.144
  83.9 0.9 broadcast_bitcast_fusion.2
  84.8 2.3 %fusion.47 = f32[32,32,32]{1,0,2:T(8,128)S(1)} fusion(f32[32,32,32]{1,2,0:T(8,128)} %broadcast_bitcast_fusion.2, f32[32,32,32]{1,2,0:T(8,128)S(1)} %get-tuple-element.44, f32[32]{0:T(128)S(1)} %broadcast_in_dim.16, f32[32,32,32]{1,0,2:T(8,128)S(1)} %get-tuple-element.19, f32[32,32,32]{1,2,0:T(8,128)S(1)} %get-tuple-element.45), kind=kLoop, calls=%fused_computation.105 | loop fusion | flops 294912 | bytes 655488 | tf_op jit(solution)/shard_map/transpose(jvp())/div | solution.py:23
  87.7 1.4 %fusion.46 = (f32[32,32,32]{1,0,2:T(8,128)S(1)}, f32[32,32,32]{1,0,2:T(8,128)S(1)}) fusion(f32[32,32,32]{1,2,0:T(8,128)S(1)} %broadcast_bitcast_fusion.1, f32[32,32,32]{1,2,0:T(8,128)S(1)} %copy-done.3, f32[32,32,32]{1,0,2:T(8,128)S(1)} %copy-done.1, f32[32,32,32]{1,2,0:T(8,128)S(1)} %copy-done.5, f32[32,32,32]{1,0,2:T(8,128)S(1)} %fusion.47, ...), kind=kLoop, calls=%fused_computation.103 | loop fusion | flops 524288 | bytes 1048576 | tf_op jit(solution)/shard_map/transpose(jvp())/div | solution.py:23
  89.7 1.5 %fusion.45 = (f32[32,32,32]{1,0,2:T(8,128)S(1)}, f32[32,32,32]{1,0,2:T(8,128)S(1)}) fusion(f32[32,32,32]{1,2,0:T(8,128)S(1)} %broadcast_bitcast_fusion, f32[32,32,32]{1,2,0:T(8,128)S(1)} %get-tuple-element.40, f32[32,32,32]{1,0,2:T(8,128)S(1)} %get-tuple-element.27, f32[32,32,32]{1,2,0:T(8,128)S(1)} %get-tuple-element.41, ...), kind=kLoop, calls=%fused_computation.101 | loop fusion | flops 524288 | bytes 1048576 | tf_op jit(solution)/shard_map/transpose(jvp())/div | solution.py:23
  91.2 0.8 fusion.43
  92.1 0.8 fusion.39
  94.3 0.8 fusion.31
  95.3 1.1 copy.180
  96.4 11.1 %fusion.156 = f32[1024,4,3]{1,2,0:T(4,128)} fusion(f32[1024,4,8]{2,1,0:T(4,128)S(1)} %copy.180, f32[8,3,1024]{1,0,2:T(8,128)} %copy.149), kind=kOutput, calls=%fused_computation.323 | convolution fusion | flops 1179648 | bytes 278528 | tf_op jit(solution)/shard_map/transpose(jvp(scp,tcp->pst))/dot_general | solution.py:44
  107.5 1.8 %copy.182 = f32[1024,4,3]{0,1,2:T(4,128)S(1)} copy(f32[1024,4,3]{1,2,0:T(4,128)} %fusion.156) | data formatting | bytes 98304 | tf_op jit(solution)/shard_map/transpose(jvp(scp,tcp->pst))/dot_general | solution.py:44
  109.5 16.1 %all-reduce.63 = f32[4,3,1024]{2,1,0:T(4,128)S(1)} all-reduce(f32[4,3,1024]{2,1,0:T(4,128)S(1)} %copy.192), channel_id=2, replica_groups=mesh['tgt'=4,'sup'=8] {'tgt'}, use_global_device_ids=true, to_apply=%region_7.8.clone | all-reduce | flops 12288 | bytes 98304
  125.5 0.6 dynamic-slice
  126.1 0.7 constant_dynamic-slice_fusion
  126.8 0.6 copy.193
  (96 shorter events, 7.3 us)
Async XLA Ops:
  0.6 55.1 %copy-start = (f32[4,100]{1,0:T(4,128)S(1)}, f32[4,100]{1,0:T(4,128)}, u32[]{:S(2)}) copy-start(f32[4,100]{1,0:T(4,128)} %param.5) | copy-start | bytes 4804
  0.6 11.3 %copy-start.20 = (f32[1,3,1024]{2,0,1:T(1,128)S(1)}, f32[1,3,1024]{2,0,1:T(1,128)}, u32[]{:S(2)}) copy-start(f32[1,3,1024]{2,0,1:T(1,128)} %param.6) | copy-start | bytes 36868
  11.1 19.5 %copy-start.6 = (f32[4,3,1024]{2,1,0:T(4,128)}, f32[4,3,1024]{2,1,0:T(4,128)S(1)}, u32[]{:S(2)}) copy-start(f32[4,3,1024]{2,1,0:T(4,128)S(1)} %all_gather.9) | copy-start | bytes 147460
  11.9 34.0 %copy-start.8 = (f32[32,32,4]{1,0,2:T(8,128)}, f32[32,32,4]{1,0,2:T(8,128)S(1)}, u32[]{:S(2)}) copy-start(f32[32,32,4]{1,0,2:T(8,128)S(1)} %get-tuple-element.29) | copy-start | bytes 49156
  12.0 15.9 %copy-start.12 = (f32[32,32,4]{1,2,0:T(4,128)}, f32[32,32,4]{1,2,0:T(4,128)S(1)}, u32[]{:S(2)}) copy-start(f32[32,32,4]{1,2,0:T(4,128)S(1)} %copy.155) | copy-start | bytes 49156
  43.0 3.9 %copy-start.17 = (f32[32,32,8]{1,0,2:T(8,128)S(1)}, f32[32,32,8]{1,0,2:T(8,128)}, u32[]{:S(2)}) copy-start(f32[32,32,8]{1,0,2:T(8,128)} %get-tuple-element.31) | copy-start | bytes 98308
  46.8 4.2 %copy-start.10 = (f32[32,32,4]{1,0,2:T(8,128)}, f32[32,32,4]{1,0,2:T(8,128)S(1)}, u32[]{:S(2)}) copy-start(f32[32,32,4]{1,0,2:T(8,128)S(1)} %get-tuple-element.25) | copy-start | bytes 49156
  46.9 4.1 %copy-start.14 = (f32[32,32,4]{1,2,0:T(4,128)}, f32[32,32,4]{1,2,0:T(4,128)S(1)}, u32[]{:S(2)}) copy-start(f32[32,32,4]{1,2,0:T(4,128)S(1)} %copy.163) | copy-start | bytes 49156
  47.7 5.7 %copy-start.2 = (f32[32,32,32]{1,2,0:T(8,128)}, f32[32,32,32]{1,2,0:T(8,128)S(1)}, u32[]{:S(2)}) copy-start(f32[32,32,32]{1,2,0:T(8,128)S(1)} %get-tuple-element.42) | copy-start | bytes 393220
  47.7 5.7 %copy-start.4 = (f32[32,32,32]{1,2,0:T(8,128)}, f32[32,32,32]{1,2,0:T(8,128)S(1)}, u32[]{:S(2)}) copy-start(f32[32,32,32]{1,2,0:T(8,128)S(1)} %get-tuple-element.43) | copy-start | bytes 393220
  52.6 3.1 %copy-start.16 = (f32[32,32,4]{1,2,0:T(4,128)}, f32[32,32,4]{1,2,0:T(4,128)S(1)}, u32[]{:S(2)}) copy-start(f32[32,32,4]{1,2,0:T(4,128)S(1)} %copy.167) | copy-start | bytes 49156
  52.6 20.2 %copy-start.21 = (f32[1,100]{1,0:T(1,128)S(1)}, f32[1,100]{1,0:T(1,128)}, u32[]{:S(2)}) copy-start(f32[1,100]{1,0:T(1,128)} %param.7) | copy-start | bytes 1204
  83.9 3.6 %copy-start.19 = (f32[32,32,4]{1,0,2:T(8,128)S(1)}, f32[32,32,4]{1,0,2:T(8,128)}, u32[]{:S(2)}) copy-start(f32[32,32,4]{1,0,2:T(8,128)} %get-tuple-element.37) | copy-start | bytes 49156
  84.8 2.8 %copy-start.1 = (f32[32,32,32]{1,0,2:T(8,128)S(1)}, f32[32,32,32]{1,0,2:T(8,128)}, u32[]{:S(2)}) copy-start(f32[32,32,32]{1,0,2:T(8,128)} %get-tuple-element.23) | copy-start | bytes 393220
  84.8 2.8 %copy-start.3 = (f32[32,32,32]{1,2,0:T(8,128)S(1)}, f32[32,32,32]{1,2,0:T(8,128)}, u32[]{:S(2)}) copy-start(f32[32,32,32]{1,2,0:T(8,128)} %copy-done.2) | copy-start | bytes 393220
  84.8 2.8 %copy-start.5 = (f32[32,32,32]{1,2,0:T(8,128)S(1)}, f32[32,32,32]{1,2,0:T(8,128)}, u32[]{:S(2)}) copy-start(f32[32,32,32]{1,2,0:T(8,128)} %copy-done.4) | copy-start | bytes 393220
  87.7 1.9 %copy-start.18 = (f32[32,32,4]{1,0,2:T(8,128)S(1)}, f32[32,32,4]{1,0,2:T(8,128)}, u32[]{:S(2)}) copy-start(f32[32,32,4]{1,0,2:T(8,128)} %get-tuple-element.39) | copy-start | bytes 49156
  89.7 1.6 %copy-start.13 = (f32[32,32,4]{1,2,0:T(4,128)S(1)}, f32[32,32,4]{1,2,0:T(4,128)}, u32[]{:S(2)}) copy-start(f32[32,32,4]{1,2,0:T(4,128)} %copy-done.12) | copy-start | bytes 49156
  89.7 2.4 %copy-start.15 = (f32[32,32,4]{1,2,0:T(4,128)S(1)}, f32[32,32,4]{1,2,0:T(4,128)}, u32[]{:S(2)}) copy-start(f32[32,32,4]{1,2,0:T(4,128)} %copy-done.14) | copy-start | bytes 49156
  91.2 1.8 %copy-start.11 = (f32[32,32,4]{1,0,2:T(8,128)S(1)}, f32[32,32,4]{1,0,2:T(8,128)}, u32[]{:S(2)}) copy-start(f32[32,32,4]{1,0,2:T(8,128)} %copy-done.10) | copy-start | bytes 49156
  91.2 2.1 %copy-start.9 = (f32[32,32,4]{1,0,2:T(8,128)S(1)}, f32[32,32,4]{1,0,2:T(8,128)}, u32[]{:S(2)}) copy-start(f32[32,32,4]{1,0,2:T(8,128)} %copy-done.8) | copy-start | bytes 49156
  107.5 1.8 %copy-start.7 = (f32[4,3,1024]{2,1,0:T(4,128)S(1)}, f32[4,3,1024]{2,1,0:T(4,128)}, u32[]{:S(2)}) copy-start(f32[4,3,1024]{2,1,0:T(4,128)} %copy-done.6) | copy-start | bytes 147460
  107.5 18.0 %copy-start.22 = (u32[32]{0:T(128)S(1)}, u32[32]{0:T(128)}, u32[]{:S(2)}) copy-start(u32[32]{0:T(128)} %constant.232) | copy-start | bytes 388
where the time goes:
time: 128 us
  blocking collectives  65.5 us (51%)
  other arithmetic  25.1 us (20%)
  matrix products  21.2 us (17%)
  local copies, waits for them, and re-layouts  14.8 us (12%)
    dot_general x2, matrix products, pair_kernel(): jnp.einsum('scp,tcp->pst', support, targets, precision=lax.Precision.HIGH...  20.9 us
    psum x1, blocking collectives, local(): predicted = lax.psum(product(theta.T, coeffs), 'sup')  16.9 us
    unnamed x1, blocking collectives  16.1 us
    all_gather x1, blocking collectives, local(): lax.all_gather(targets, 'sup', axis=0, tiled=True)  14.3 us
    all_gather x1, blocking collectives, local(): block = lax.all_gather(support, 'tgt', axis=0, tiled=True)  9.71 us
    all_gather x1, blocking collectives, local(): lax.all_gather(labels, 'sup', axis=0, tiled=True)  8.65 us
    div x6, other arithmetic, spread(): return summed / 9.0  6.42 us
    mul x2, other arithmetic, pair_kernel(): activated = 2.0 / math.pi * jnp.arcsin(correlation)  6 us

commit v1 on v0

--- a/solution.py
+++ b/solution.py
@@ -8,6 +8,11 @@
 DEPTH = 3
 WEIGHT_VAR = 1.6
 BIAS_VAR = 0.1
+
+
+def gather_by_exchange(value, axis, dim):
+    copies = jnp.concatenate([value] * lax.axis_size(axis), axis=dim)
+    return lax.all_to_all(copies, axis, dim, dim, tiled=True)
 
 
 def spread(values):
@@ -74,7 +79,7 @@
     block = lax.all_gather(support, "tgt", axis=0, tiled=True)
     group, group_labels = (
         lax.all_gather(targets, "sup", axis=0, tiled=True),
-        lax.all_gather(labels, "sup", axis=0, tiled=True),
+        gather_by_exchange(labels, "sup", 0),
     )
     theta, pullback = jax.vjp(lambda images: pair_kernel(images, group), block)
     predicted = lax.psum(product(theta.T, coeffs), "sup")

time: 128 us -> 127 us (level)
  blocking collectives: 65.5 us -> 53.9 us
  starting transfers between devices: 0 us -> 6.35 us
  local copies, waits for them, and re-layouts: 14.8 us -> 20.6 us
  other arithmetic: 25.1 us -> 23.2 us
    all_gather x1 -> x0, blocking collectives: 8.65 us -> none  [local(): lax.all_gather(labels, 'sup', axis=0, tiled=True)]
    all_to_all x0 -> x1, starting transfers between devices: none -> 6.35 us  [gather_by_exchange(): return lax.all_to_all(copies, axis, dim, dim, tiled=True)]
    psum x1, blocking collectives: 16.9 us -> 15 us  [local(): predicted = lax.psum(product(theta.T, coeffs), 'sup')]
    rsqrt x3, local copies, waits for them, and re-layouts: 0.14 us -> 1.82 us  [pair_kernel(): sup_gain = lax.rsqrt(1.0 + 2.0 * sup_levels[layer_idx])]
    all_gather x1, blocking collectives: 9.71 us -> 8.24 us  [local(): block = lax.all_gather(support, 'tgt', axis=0, tiled=True)]
    mul x9, local copies, waits for them, and re-layouts: 1.35 us -> 2.79 us  [pair_kernel(): 2.0 * kernel_level.reshape(SIDE, SIDE, sup_count, tgt_count)]
    div x6, other arithmetic: 6.42 us -> 5.12 us  [spread(): return summed / 9.0]
    unnamed x53 -> x47, local copies, waits for them, and re-layouts: 3.1 us -> 4.3 us
  transfers between devices with their start and end apart: 0 -> 1, of which waited for: 0 -> 0; matrix products, arithmetic and copies ran while one was open for 0% -> 28% of each run, Pallas kernels for 0% -> 0%
where the time goes in v1:
time: 127 us
  blocking collectives  53.9 us (42%)
  other arithmetic  23.2 us (18%)
  matrix products  21.2 us (17%)
  local copies, waits for them, and re-layouts  20.6 us (16%)
  starting transfers between devices  6.35 us (5%)
    dot_general x2, matrix products, pair_kernel(): jnp.einsum('scp,tcp->pst', support, targets, precision=lax.Precision.HIGH...  20.8 us
    unnamed x1, blocking collectives  16.2 us
    psum x1, blocking collectives, local(): predicted = lax.psum(product(theta.T, coeffs), 'sup')  15 us
    all_gather x1, blocking collectives, local(): lax.all_gather(targets, 'sup', axis=0, tiled=True)  14.5 us
    all_gather x1, blocking collectives, local(): block = lax.all_gather(support, 'tgt', axis=0, tiled=True)  8.24 us
    all_to_all x1, starting transfers between devices, gather_by_exchange(): return lax.all_to_all(copies, axis, dim, dim, tiled=True)  6.35 us
    mul x2, other arithmetic, pair_kernel(): activated = 2.0 / math.pi * jnp.arcsin(correlation)  5.96 us
    div x6, other arithmetic, spread(): return summed / 9.0  5.12 us
  transfers between devices with their start and end apart: 1, of which 0 were waited for; matrix products, arithmetic and copies ran while one was open for 28% of the time, Pallas kernels for 0%

profile of v1, /device:TPU:0, one launch (start us, length us, event | category | flops | bytes accessed | tf_op | source)
XLA Modules:
  0.0 126.5 jit_solution(16598067106635339634)
XLA Ops:
  0.6 1.3 concatenate.3
  1.9 6.4 %all-to-all-start = ((f32[8,1,100]{2,1,0:T(1,128)}), f32[8,1,100]{2,1,0:T(1,128)S(1)}, u32[]{:S(2)}, u32[]{:S(2)}) async-start(f32[8,1,100]{2,1,0:T(1,128)} %concatenate.3), calls=%async_computation | async-start | bytes 8192 | tf_op jit(solution)/shard_map/all_to_all | solution.py:15
  9.0 14.5 %all_gather.7 = f32[8,3,1024]{2,1,0:T(4,128)S(1)} all-gather(f32[1,3,1024]{2,1,0:T(4,128)S(1)} %copy.144), channel_id=1, replica_groups=mesh['tgt'=4,'sup'=8] {'sup'}, dimensions={0}, use_global_device_ids=true | all-gather | bytes 110592 | tf_op jit(solution)/shard_map/all_gather | solution.py:81
  23.5 2.7 %copy.146 = f32[8,3,1024]{1,0,2:T(8,128)} copy(f32[8,3,1024]{2,1,0:T(4,128)S(1)} %all_gather.7) | data formatting | bytes 196608 | tf_op jit(solution)/shard_map/all_gather | solution.py:81
  26.2 8.2 %all_gather.6 = f32[4,3,1024]{2,1,0:T(4,128)S(1)} all-gather(f32[1,3,1024]{2,1,0:T(4,128)S(1)} %copy.143), channel_id=1, replica_groups=mesh['tgt'=4,'sup'=8] {'tgt'}, dimensions={0}, use_global_device_ids=true | all-gather | bytes 61440 | tf_op jit(solution)/shard_map/all_gather | solution.py:79
  35.1 0.9 copy.145
  38.3 9.7 %convolution_multiply_fusion = f32[1024,4,8]{2,1,0:T(4,128)} fusion(f32[4,3,1024]{1,0,2:T(4,128)S(1)} %copy.145, f32[8,3,1024]{1,0,2:T(8,128)} %copy.146), kind=kOutput, calls=%fused_computation | convolution fusion | flops 1212416 | bytes 278528 | tf_op jit(solution)/shard_map/jvp(scp,tcp->pst)/dot_general | solution.py:49
  48.0 2.0 %copy.147 = f32[1024,4,8]{0,2,1:T(8,128)S(1)} copy(f32[1024,4,8]{2,1,0:T(4,128)} %convolution_multiply_fusion) | data formatting | bytes 262144 | tf_op jit(solution)/shard_map/jvp()/div | solution.py:49
  50.2 0.7 add_multiply_fusion.11
  51.8 0.8 add_multiply_fusion.9
  52.6 0.8 broadcast_multiply_fusion.2
  54.4 3.3 %add_multiply_fusion.3 = (f32[32,32,32]{1,0,2:T(8,128)S(1)}, f32[32,32,32]{1,0,2:T(8,128)}) fusion(f32[32,32,32]{1,2,0:T(8,128)S(1)} %get-tuple-element.40, f32[32,32,32]{1,2,0:T(8,128)S(1)} %get-tuple-element.41, f32[32,32,32]{1,0,2:T(8,128)S(1)} %reshape.85), kind=kLoop, calls=%fused_computation.116 | loop fusion | flops 589824 | bytes 655360 | tf_op jit(solution)/shard_map/jvp()/mul | solution.py:65
  57.8 2.7 %add_multiply_fusion.1 = (f32[32,32,32]{1,0,2:T(8,128)S(1)}, f32[32,32,32]{1,0,2:T(8,128)S(1)}) fusion(f32[32,32,32]{1,2,0:T(8,128)S(1)} %get-tuple-element.42, f32[32,32,32]{1,2,0:T(8,128)S(1)} %get-tuple-element.43, f32[32,32,32]{1,0,2:T(8,128)S(1)} %get-tuple-element.26), kind=kLoop, calls=%fused_computation.114 | loop fusion | flops 589824 | bytes 655360 | tf_op jit(solution)/shard_map/jvp()/mul | solution.py:65
  60.4 2.3 %multiply_reduce_fusion = (f32[32]{0:T(128)S(1)}, f32[32,32,32]{1,0,2:T(8,128)S(1)}) fusion(f32[32,32,32]{1,2,0:T(8,128)S(1)} %get-tuple-element.44, f32[32,32,32]{1,2,0:T(8,128)S(1)} %get-tuple-element.45, f32[32,32,32]{1,0,2:T(8,128)S(1)} %get-tuple-element.22), kind=kLoop, calls=%fused_computation.112 | loop fusion | flops 622560 | bytes 524416 | tf_op jit(solution)/shard_map/jvp()/reduce_sum | solution.py:70
  62.8 0.9 copy.172
  63.7 0.9 broadcast_bitcast_fusion.1
  64.5 0.9 copy.175
  65.4 0.9 broadcast_bitcast_fusion
  66.5 1.2 dynamic-slice
  67.7 15.0 %psum.7 = f32[8,100]{1,0:T(8,128)S(1)} all-reduce(f32[8,100]{1,0:T(8,128)S(1)} %fusion.155), channel_id=1, replica_groups=mesh['tgt'=4,'sup'=8] {'sup'}, use_global_device_ids=true, to_apply=%region_3.4 | all-reduce | flops 800 | bytes 6400 | tf_op jit(solution)/shard_map/psum | solution.py:85
  83.0 1.4 %fusion.35 = f32[32,32,4]{1,2,0:T(4,128)S(1)} fusion(f32[32,32,32]{1,0,2:T(8,128)S(1)} %get-tuple-element.19, f32[4,8]{1,0:T(4,128)S(1)} %fusion, f32[32,32,8]{1,2,0:T(8,128)S(1)} %copy.166, f32[32,32,4]{1,2,0:T(4,128)} %copy-done.18), kind=kLoop, calls=%fused_computation.84 | loop fusion | flops 323584 | bytes 196736 | tf_op jit(solution)/shard_map/transpose(jvp())/reduce_sum | solution.py:60
  84.3 0.9 fusion.144
  85.4 0.9 fusion.47
  86.8 1.5 %fusion.46 = (f32[32,32,32]{1,0,2:T(8,128)S(1)}, f32[32,32,32]{1,0,2:T(8,128)S(1)}) fusion(f32[32,32,32]{1,2,0:T(8,128)S(1)} %copy-done.7, f32[32,32,32]{1,2,0:T(8,128)S(1)} %copy-done.3, f32[32,32,32]{1,0,2:T(8,128)S(1)} %get-tuple-element.23, f32[32,32,32]{1,2,0:T(8,128)S(1)} %copy-done.5, f32[32,32,32]{1,0,2:T(8,128)S(1)} %fusion.47, ...), kind=kLoop, calls=%fused_computation.103 | loop fusion | flops 524288 | bytes 1048576 | tf_op jit(solution)/shard_map/transpose(jvp())/div | solution.py:28
  88.7 1.5 %fusion.45 = (f32[32,32,32]{1,0,2:T(8,128)S(1)}, f32[32,32,32]{1,0,2:T(8,128)S(1)}) fusion(f32[32,32,32]{1,2,0:T(8,128)S(1)} %copy-done.6, f32[32,32,32]{1,2,0:T(8,128)S(1)} %get-tuple-element.40, f32[32,32,32]{1,0,2:T(8,128)S(1)} %copy-done.1, f32[32,32,32]{1,2,0:T(8,128)S(1)} %get-tuple-element.41, f32[32,32,32]{1,0,2:T(8,128)S(1)} %get-tuple-element.16, ...), kind=kLoop, calls=%fused_computation.101 | loop fusion | flops 524288 | bytes 1048576 | tf_op jit(solution)/shard_map/transpose(jvp())/div | solution.py:28
  90.2 0.8 fusion.43
  91.1 0.8 fusion.39
  93.3 0.8 fusion.31
  94.3 1.1 copy.177
  95.4 11.1 %fusion.156 = f32[1024,4,3]{1,2,0:T(4,128)} fusion(f32[1024,4,8]{2,1,0:T(4,128)S(1)} %copy.177, f32[8,3,1024]{1,0,2:T(8,128)} %copy.146), kind=kOutput, calls=%fused_computation.323 | convolution fusion | flops 1179648 | bytes 278528 | tf_op jit(solution)/shard_map/transpose(jvp(scp,tcp->pst))/dot_general | solution.py:49
  106.5 1.8 %copy.179 = f32[1024,4,3]{0,1,2:T(4,128)S(1)} copy(f32[1024,4,3]{1,2,0:T(4,128)} %fusion.156) | data formatting | bytes 98304 | tf_op jit(solution)/shard_map/transpose(jvp(scp,tcp->pst))/dot_general | solution.py:49
  108.5 16.2 %all-reduce.63 = f32[4,3,1024]{2,1,0:T(4,128)S(1)} all-reduce(f32[4,3,1024]{2,1,0:T(4,128)S(1)} %copy.189), channel_id=2, replica_groups=mesh['tgt'=4,'sup'=8] {'tgt'}, use_global_device_ids=true, to_apply=%region_7.8.clone | all-reduce | flops 12288 | bytes 98304
  (92 shorter events, 10.6 us)
Async XLA Ops:
  0.6 65.7 %copy-start = (f32[4,100]{1,0:T(4,128)S(1)}, f32[4,100]{1,0:T(4,128)}, u32[]{:S(2)}) copy-start(f32[4,100]{1,0:T(4,128)} %param.5) | copy-start | bytes 4804
  1.9 80.8 %all-to-all-start = ((f32[8,1,100]{2,1,0:T(1,128)}), f32[8,1,100]{2,1,0:T(1,128)S(1)}, u32[]{:S(2)}, u32[]{:S(2)}) async-start(f32[8,1,100]{2,1,0:T(1,128)} %concatenate.3), calls=%async_computation | async-start | bytes 8192 | tf_op jit(solution)/shard_map/all_to_all | solution.py:15
  23.5 2.7 %copy-start.19 = (f32[1,3,1024]{2,0,1:T(1,128)S(1)}, f32[1,3,1024]{2,0,1:T(1,128)}, u32[]{:S(2)}) copy-start(f32[1,3,1024]{2,0,1:T(1,128)} %param.4) | copy-start | bytes 36868
  34.5 0.6 copy-start.8
  36.7 13.4 %copy-start.10 = (f32[32,32,4]{1,0,2:T(8,128)}, f32[32,32,4]{1,0,2:T(8,128)S(1)}, u32[]{:S(2)}) copy-start(f32[32,32,4]{1,0,2:T(8,128)S(1)} %get-tuple-element.29) | copy-start | bytes 49156
  50.0 4.2 %copy-start.14 = (f32[32,32,4]{1,2,0:T(4,128)S(1)}, f32[32,32,4]{1,2,0:T(4,128)}, u32[]{:S(2)}) copy-start(f32[32,32,4]{1,2,0:T(4,128)} %copy.152) | copy-start | bytes 49156
  51.1 3.2 %copy-start.12 = (f32[32,32,4]{1,0,2:T(8,128)}, f32[32,32,4]{1,0,2:T(8,128)S(1)}, u32[]{:S(2)}) copy-start(f32[32,32,4]{1,0,2:T(8,128)S(1)} %get-tuple-element.25) | copy-start | bytes 49156
  51.1 3.1 %copy-start.16 = (f32[32,32,4]{1,2,0:T(4,128)}, f32[32,32,4]{1,2,0:T(4,128)S(1)}, u32[]{:S(2)}) copy-start(f32[32,32,4]{1,2,0:T(4,128)S(1)} %copy.160) | copy-start | bytes 49156
  53.4 1.0 copy-start.18
  54.3 6.1 %copy-start.2 = (f32[32,32,32]{1,2,0:T(8,128)}, f32[32,32,32]{1,2,0:T(8,128)S(1)}, u32[]{:S(2)}) copy-start(f32[32,32,32]{1,2,0:T(8,128)S(1)} %get-tuple-element.42) | copy-start | bytes 393220
  54.3 6.1 %copy-start.4 = (f32[32,32,32]{1,2,0:T(8,128)}, f32[32,32,32]{1,2,0:T(8,128)S(1)}, u32[]{:S(2)}) copy-start(f32[32,32,32]{1,2,0:T(8,128)S(1)} %get-tuple-element.43) | copy-start | bytes 393220
  85.3 1.5 %copy-start.3 = (f32[32,32,32]{1,2,0:T(8,128)S(1)}, f32[32,32,32]{1,2,0:T(8,128)}, u32[]{:S(2)}) copy-start(f32[32,32,32]{1,2,0:T(8,128)} %copy-done.2) | copy-start | bytes 393220
  85.3 1.5 %copy-start.5 = (f32[32,32,32]{1,2,0:T(8,128)S(1)}, f32[32,32,32]{1,2,0:T(8,128)}, u32[]{:S(2)}) copy-start(f32[32,32,32]{1,2,0:T(8,128)} %copy-done.4) | copy-start | bytes 393220
  85.3 1.5 %copy-start.7 = (f32[32,32,32]{1,2,0:T(8,128)S(1)}, f32[32,32,32]{1,2,0:T(8,128)}, u32[]{:S(2)}) copy-start(f32[32,32,32]{1,2,0:T(8,128)} %broadcast_bitcast_fusion.1) | copy-start | bytes 393220
  86.8 1.9 %copy-start.1 = (f32[32,32,32]{1,0,2:T(8,128)S(1)}, f32[32,32,32]{1,0,2:T(8,128)}, u32[]{:S(2)}) copy-start(f32[32,32,32]{1,0,2:T(8,128)} %get-tuple-element.27) | copy-start | bytes 393220
  86.8 1.9 %copy-start.6 = (f32[32,32,32]{1,2,0:T(8,128)S(1)}, f32[32,32,32]{1,2,0:T(8,128)}, u32[]{:S(2)}) copy-start(f32[32,32,32]{1,2,0:T(8,128)} %broadcast_bitcast_fusion) | copy-start | bytes 393220
  88.7 1.6 %copy-start.15 = (f32[32,32,4]{1,2,0:T(4,128)S(1)}, f32[32,32,4]{1,2,0:T(4,128)}, u32[]{:S(2)}) copy-start(f32[32,32,4]{1,2,0:T(4,128)} %copy.152) | copy-start | bytes 49156
  88.7 2.4 %copy-start.17 = (f32[32,32,4]{1,2,0:T(4,128)S(1)}, f32[32,32,4]{1,2,0:T(4,128)}, u32[]{:S(2)}) copy-start(f32[32,32,4]{1,2,0:T(4,128)} %copy-done.16) | copy-start | bytes 49156
  90.2 1.8 %copy-start.13 = (f32[32,32,4]{1,0,2:T(8,128)S(1)}, f32[32,32,4]{1,0,2:T(8,128)}, u32[]{:S(2)}) copy-start(f32[32,32,4]{1,0,2:T(8,128)} %copy-done.12) | copy-start | bytes 49156
  90.2 2.1 %copy-start.11 = (f32[32,32,4]{1,0,2:T(8,128)S(1)}, f32[32,32,4]{1,0,2:T(8,128)}, u32[]{:S(2)}) copy-start(f32[32,32,4]{1,0,2:T(8,128)} %copy-done.10) | copy-start | bytes 49156
  106.5 1.8 %copy-start.9 = (f32[4,3,1024]{2,1,0:T(4,128)S(1)}, f32[4,3,1024]{2,1,0:T(4,128)}, u32[]{:S(2)}) copy-start(f32[4,3,1024]{2,1,0:T(4,128)} %copy-done.8) | copy-start | bytes 147460
